TPU v7x, 512 devices: a whole 4x4x16 slice. The times are simulated.
512 devices in a mesh: seq: 64 (over z, y), dp: 8 (over x, core).
Axes of the slice: x: 4, y: 4, z: 16, core: 2. Of those that a mesh axis runs over, the one named last changes fastest.
Arguments:
- queries: bfloat16 [8, 8192, 2048], P('dp', 'seq'), may hold values from -40 to 40
- keys: bfloat16 [8, 8192, 2048], P('dp', 'seq'), may hold values from -6 to 6
- values: bfloat16 [8, 8192, 2048], P('dp', 'seq'), may hold values from -6 to 6
- grad_out: bfloat16 [8, 8192, 2048], P('dp', 'seq'), may hold values from -48 to 48
- lengths: int32 [8], P('dp'), may hold values from 1024 to 8192, as said below
- fields: int32 [8, 8192], P('dp', 'seq'), may hold values from 0 to 63
- field_bias: bfloat16 [16, 64], replicated, may hold values from -6 to 6
Outputs:
- grad_queries: bfloat16 [8, 8192, 2048], P('dp', 'seq')
- grad_keys: bfloat16 [8, 8192, 2048], P('dp', 'seq')
- grad_values: bfloat16 [8, 8192, 2048], P('dp', 'seq')
- grad_bias: float32 [16, 64], replicated
Inputs may be any that keep to these rules, and one draw needn't show every extreme that they name: `lengths`: the valid positions of a sequence form a prefix; in every draw some sequence is full.
All inputs are finite; a program needn't handle non-finite values.
Results may differ from a plain program's by a relative error of at most 0.0077.
Values may be sent and summed in bfloat16 or wider, within the bound.
A program may use at most 128 MiB of HBM per device.

v0:
```python
import jax
import jax.numpy as jnp
from jax import lax
from jax.sharding import PartitionSpec as P

HEADS = 16
HEAD_DIM = 128
WINDOW = 512
FIELDS = 64


def passed_along(value, axis, steps):
    count = lax.axis_size(axis)
    first, last = (max(0, -steps), min(count, count - steps))
    return lax.ppermute(value, axis, [(source, source + steps) for source in range(first, last)])


def split_heads(rows):
    return rows.reshape(rows.shape[0], HEADS, HEAD_DIM)


def band_mask(query_places, key_places, length):
    not_after = key_places[None, :] <= query_places[:, None]
    inside = key_places[None, :] > query_places[:, None] - WINDOW
    started = key_places[None, :] >= 0
    live_rows = query_places[:, None] < length
    return not_after & inside & started & live_rows


def logits_of(query_heads, key_heads, key_bias):
    factor = HEAD_DIM ** (-0.5)
    products = jnp.einsum(
        "qhd,khd->hqk", query_heads, key_heads, preferred_element_type=jnp.float32
    )
    return products * factor + key_bias[:, None, :]


def grad_logits_of(attn_weights, row_delta, grad_heads, value_heads):
    grad_probs = jnp.einsum(
        "qhd,khd->hqk", grad_heads, value_heads, preferred_element_type=jnp.float32
    )
    return attn_weights * (grad_probs - row_delta[:, :, None])


def shards(queries, keys, values, grad_out, lengths, fields, field_bias):
    tok_rows = queries.shape[1]
    row_width = queries.shape[2]
    length = lengths[0]
    query_own = queries[0]
    key_own = keys[0]
    value_own = values[0]
    grad_own = grad_out[0]
    reach_blocks = WINDOW // tok_rows
    factor = HEAD_DIM ** (-0.5)
    block_index = lax.axis_index("seq")
    onehot = (fields[0][:, None] == jnp.arange(FIELDS, dtype=jnp.int32)[None, :]).astype(
        jnp.bfloat16
    )
    own_bias = jnp.dot(field_bias, onehot.T, preferred_element_type=jnp.float32).astype(
        jnp.bfloat16
    )
    package = (key_own, value_own, own_bias)
    arrived = []
    for distance in range(1, reach_blocks + 1):
        arrived.append(passed_along((package[0], package[1], package[2]), "seq", distance))
    ordered = arrived[::-1] + [package]
    key_all = jnp.concatenate([arrival[0] for arrival in ordered], axis=0)
    value_all = jnp.concatenate([arrival[1] for arrival in ordered], axis=0)
    bias_all = jnp.concatenate([arrival[2] for arrival in ordered], axis=1).astype(jnp.float32)
    query_places = block_index * tok_rows + jnp.arange(tok_rows, dtype=jnp.int32)
    key_places = (block_index - reach_blocks) * tok_rows + jnp.arange(
        (reach_blocks + 1) * tok_rows, dtype=jnp.int32
    )
    query_heads = split_heads(query_own)
    grad_heads = split_heads(grad_own)
    key_heads = split_heads(key_all)
    value_heads = split_heads(value_all)
    logits = logits_of(query_heads, key_heads, bias_all)
    visible = band_mask(query_places, key_places, length)[None]
    live_rows = (query_places < length)[None, :, None]
    row_peak = jnp.max(jnp.where(visible, logits, -1e30), axis=2, keepdims=True)
    powers = jnp.where(visible, jnp.exp(logits - row_peak), 0.0)
    totals = jnp.where(live_rows, jnp.sum(powers, axis=2, keepdims=True), 1.0)
    attn_weights = powers / totals
    weights_low = attn_weights.astype(jnp.bfloat16)
    outputs = jnp.einsum(
        "hqk,khd->qhd", weights_low, value_heads, preferred_element_type=jnp.float32
    )
    row_delta = jnp.einsum("qhd,qhd->hq", grad_heads.astype(jnp.float32), outputs)
    grad_logits = grad_logits_of(attn_weights, row_delta, grad_heads, value_heads)
    grad_low = grad_logits.astype(jnp.bfloat16)
    grad_query = (
        jnp.einsum("hqk,khd->qhd", grad_low, key_heads, preferred_element_type=jnp.float32) * factor
    )
    own_cols = reach_blocks * tok_rows
    grad_key = (
        jnp.einsum(
            "hqk,qhd->khd", grad_low, query_heads, preferred_element_type=jnp.float32
        ).reshape(-1, row_width)
        * factor
    )
    grad_value = jnp.einsum(
        "hqk,qhd->khd", weights_low, grad_heads, preferred_element_type=jnp.float32
    ).reshape(-1, row_width)
    column = jnp.sum(grad_logits, axis=1)
    key_total = grad_key[own_cols:]
    value_total = grad_value[own_cols:]
    column_total = column[:, own_cols:]
    for distance in range(1, reach_blocks + 1):
        first_row = (reach_blocks - distance) * tok_rows
        returned = passed_along(
            (
                grad_key[first_row : first_row + tok_rows],
                grad_value[first_row : first_row + tok_rows],
                column[:, first_row : first_row + tok_rows],
            ),
            "seq",
            -distance,
        )
        key_total = key_total + returned[0]
        value_total = value_total + returned[1]
        column_total = column_total + returned[2]
    bias_local = jnp.dot(column_total, onehot.astype(jnp.float32), precision=lax.Precision.HIGHEST)
    query_low = grad_query.reshape(tok_rows, row_width).astype(jnp.bfloat16)
    key_low = key_total.astype(jnp.bfloat16)
    value_low = value_total.astype(jnp.bfloat16)
    bias_total = lax.psum(bias_local, ("seq", "dp"))
    return (
        query_low.reshape(1, tok_rows, row_width),
        key_low.reshape(1, tok_rows, row_width),
        value_low.reshape(1, tok_rows, row_width),
        bias_total,
    )


def solution(mesh):
    return jax.shard_map(
        shards,
        mesh=mesh,
        in_specs=(
            P("dp", "seq", None),
            P("dp", "seq", None),
            P("dp", "seq", None),
            P("dp", "seq", None),
            P("dp"),
            P("dp", "seq"),
            P(),
        ),
        out_specs=(P("dp", "seq", None), P("dp", "seq", None), P("dp", "seq", None), P()),
        check_vma=False,
    )
```

profile of v0, /device:TPU:1, one launch (start us, length us, event | category | flops | bytes accessed | tf_op | source)
XLA Modules:
  0.0 491.5 jit_solution(1476968906301964713)
XLA Ops:
  2.2 4.2 collective-permute-start.7
  6.4 4.5 collective-permute-start.6
  10.9 1.3 copy.35
  12.2 2.6 collective-permute-start.11
  14.9 4.8 collective-permute-start.10
  19.7 4.2 collective-permute-start.9
  24.6 2.6 collective-permute-start.5
  27.3 4.8 collective-permute-start.4
  32.3 1.3 copy.27
  38.1 5.2 %collective-permute-done.5 = bf16[16,128]{1,0:T(8,128)(2,1)S(1)} collective-permute-done((bf16[16,128]{1,0:T(8,128)(2,1)S(1)}, bf16[16,128]{1,0:T(8,128)(2,1)S(1)}, u32[]{:S(2)}, u32[]{:S(2)}) %collective-permute-start.5) | collective-permute-done | bytes 4128 | tf_op jit(solution)/shard_map/ppermute | solution.py:15
  44.7 18.3 %collective-permute-start.3 = (bf16[128,2048]{0,1:T(8,128)(2,1)S(1)}, bf16[128,2048]{0,1:T(8,128)(2,1)}, u32[]{:S(2)}, u32[]{:S(2)}) collective-permute-start(bf16[128,2048]{0,1:T(8,128)(2,1)S(1)} %bitcast.102), channel_id=1, source_target_pairs={{0,8},{8,16},{16,24},{24,32},{32,40},{40,48},{48,56},{56,64},{64,7... | collective-permute-start | bytes 1572872 | tf_op jit(solution)/shard_map/ppermute | solution.py:15
  63.0 9.7 %collective-permute-start.2 = (bf16[128,2048]{0,1:T(8,128)(2,1)S(1)}, bf16[128,2048]{0,1:T(8,128)(2,1)}, u32[]{:S(2)}, u32[]{:S(2)}) collective-permute-start(bf16[128,2048]{0,1:T(8,128)(2,1)S(1)} %bitcast.103), channel_id=1, source_target_pairs={{0,16},{8,24},{16,32},{24,40},{32,48},{40,56},{48,64},{56,72},{64,... | collective-permute-start | bytes 1572872 | tf_op jit(solution)/shard_map/ppermute | solution.py:15
  72.7 5.3 %collective-permute-start.1 = (bf16[128,2048]{0,1:T(8,128)(2,1)S(1)}, bf16[128,2048]{0,1:T(8,128)(2,1)}, u32[]{:S(2)}, u32[]{:S(2)}) collective-permute-start(bf16[128,2048]{0,1:T(8,128)(2,1)S(1)} %bitcast.104), channel_id=1, source_target_pairs={{0,24},{8,32},{16,40},{24,48},{32,56},{40,64},{48,72},{56,80},{64,... | collective-permute-start | bytes 1572872 | tf_op jit(solution)/shard_map/ppermute | solution.py:15
  78.0 2.1 collective-permute-start
  82.3 2.0 copy.38
  85.4 2.0 copy.32
  87.4 2.0 copy.31
  89.5 4.0 collective-permute-done.1
  93.5 2.0 copy.30
  95.5 1.3 copy.29
  98.8 2.0 constant_dynamic-update-slice_fusion.3
  100.8 2.0 constant_dynamic-update-slice_fusion.2
  104.6 7.6 %fusion.34 = (f32[16,128]{1,0:T(8,128)S(1)}, f32[16,128,640]{1,2,0:T(8,128)}) fusion(f32[16,640]{1,0:T(8,128)S(1)} %convert_element_type.46, pred[128,640]{0,1:T(8,128)(4,1)S(1)} %and_and_fusion, bf16[640,16,128]{2,0,1:T(8,128)(2,1)} %constant_dynamic-update-slice_fusion, bf16[128,16,128]{0,2,1:T(8,128)(2,1)} %bitcast.94), kind=kOutput, calls=%fused_computation.67 | convolution fusion | flops 681575040 | bytes 8519680 | tf_op jit(solution)/shard_map/sub | solution.py:82
  115.8 1.5 copy-done.5
  117.3 3.3 fusion.8
  120.6 2.0 convolution_bitcast_fusion.1
  122.6 2.6 copy.69
  125.2 1.6 multiply_reduce_fusion
  126.9 5.2 %fusion.35 = (f32[16,640]{1,0:T(8,128)S(1)}, bf16[16,128,640]{1,2,0:T(8,128)(2,1)S(1)}) fusion(f32[16,128]{1,0:T(8,128)S(1)} %copy.70, bf16[640,16,128]{2,0,1:T(8,128)(2,1)} %copy-done.5, bf16[128,16,128]{0,2,1:T(8,128)(2,1)} %copy.55, f32[16,128,640]{1,2,0:T(8,128)} %get-tuple-element.27, f32[16,128]{1,0:T(8,128)S(1)} %broadcast_select_fusion), kind=kOutput, calls=%fused_computation.68 | convolution fusion | flops 342087680 | bytes 11067392 | tf_op jit(solution)/shard_map/qhd,khd->hqk/dot_general | solution.py:39
  133.5 2.4 fusion.32
  135.9 2.5 copy.52
  138.4 2.5 copy.51
  141.0 2.6 copy.50
  150.1 2.6 copy.53
  152.6 15.2 %collective-permute-done.20 = f32[16,128]{1,0:T(8,128)S(1)} collective-permute-done((f32[16,128]{1,0:T(8,128)S(1)}, f32[16,128]{1,0:T(8,128)S(1)}, u32[]{:S(2)}, u32[]{:S(2)}) %collective-permute-start.20) | collective-permute-done | bytes 8224 | tf_op jit(solution)/shard_map/ppermute | solution.py:15
  169.2 109.7 %collective-permute-done.23 = f32[16,128]{1,0:T(8,128)S(1)} collective-permute-done((f32[16,128]{1,0:T(8,128)S(1)}, f32[16,128]{1,0:T(8,128)S(1)}, u32[]{:S(2)}, u32[]{:S(2)}) %collective-permute-start.23) | collective-permute-done | bytes 8224 | tf_op jit(solution)/shard_map/ppermute | solution.py:15
  281.2 2.8 collective-permute-done.22
  284.0 1.5 collective-permute-start.21
  285.5 2.0 fusion.31
  287.5 1.4 copy.56
  288.8 1.4 copy.60
  290.2 2.7 copy.59
  292.9 2.6 copy.58
  300.7 2.8 fusion.11
  304.5 1.6 copy.57
  306.6 178.1 %psum.7 = f32[16,64]{1,0:T(8,128)} all-reduce(f32[16,64]{1,0:T(8,128)S(1)} %fusion.22), channel_id=1, replica_groups=mesh['seq'=64,'dp'=8] {'seq','dp'}, use_global_device_ids=true, to_apply=%region_3.4 | all-reduce | flops 1024 | bytes 8192 | tf_op jit(solution)/shard_map/psum | solution.py:127
  484.7 2.4 fusion.18
  488.1 3.4 fusion.19
  (97 shorter events, 37.5 us)
Async XLA Ops:
  0.6 0.7 copy-start
  0.6 35.0 %copy-start.12 = (bf16[1,128,2048]{2,1,0:T(8,128)(2,1)S(1)}, bf16[1,128,2048]{2,1,0:T(8,128)(2,1)}, u32[]{:S(2)}) copy-start(bf16[1,128,2048]{2,1,0:T(8,128)(2,1)} %param.7) | copy-start | bytes 1572868
  2.2 34.5 %copy-start.13 = (bf16[1,128,2048]{2,1,0:T(8,128)(2,1)S(1)}, bf16[1,128,2048]{2,1,0:T(8,128)(2,1)}, u32[]{:S(2)}) copy-start(bf16[1,128,2048]{2,1,0:T(8,128)(2,1)} %param.10) | copy-start | bytes 1572868
  2.2 22.4 %collective-permute-start.7 = (bf16[16,128]{1,0:T(8,128)(2,1)S(1)}, bf16[16,128]{1,0:T(8,128)(2,1)S(1)}, u32[]{:S(2)}, u32[]{:S(2)}) collective-permute-start(bf16[16,128]{1,0:T(8,128)(2,1)S(1)} %fusion.14), channel_id=1, source_target_pairs={{0,8},{8,16},{16,24},{24,32},{32,40},{40,48},{48,56},{56,64},{64,7... | collective-permute-start | bytes 12296 | tf_op jit(solution)/shard_map/ppermute | solution.py:15
  6.4 20.9 %collective-permute-start.6 = (bf16[16,128]{1,0:T(8,128)(2,1)S(1)}, bf16[16,128]{1,0:T(8,128)(2,1)S(1)}, u32[]{:S(2)}, u32[]{:S(2)}) collective-permute-start(bf16[16,128]{1,0:T(8,128)(2,1)S(1)} %fusion.14), channel_id=1, source_target_pairs={{0,16},{8,24},{16,32},{24,40},{32,48},{40,56},{48,64},{56,72},{64,... | collective-permute-start | bytes 12296 | tf_op jit(solution)/shard_map/ppermute | solution.py:15
  12.2 50.8 %collective-permute-start.11 = (bf16[128,2048]{0,1:T(8,128)(2,1)S(1)}, bf16[128,2048]{0,1:T(8,128)(2,1)S(1)}, u32[]{:S(2)}, u32[]{:S(2)}) collective-permute-start(bf16[128,2048]{0,1:T(8,128)(2,1)S(1)} %bitcast.96), channel_id=1, source_target_pairs={{0,8},{8,16},{16,24},{24,32},{32,40},{40,48},{48,56},{56,64},{64,7... | collective-permute-start | bytes 1572872 | tf_op jit(solution)/shard_map/ppermute | solution.py:15
  14.9 57.8 %collective-permute-start.10 = (bf16[128,2048]{0,1:T(8,128)(2,1)S(1)}, bf16[128,2048]{0,1:T(8,128)(2,1)S(1)}, u32[]{:S(2)}, u32[]{:S(2)}) collective-permute-start(bf16[128,2048]{0,1:T(8,128)(2,1)S(1)} %bitcast.97), channel_id=1, source_target_pairs={{0,16},{8,24},{16,32},{24,40},{32,48},{40,56},{48,64},{56,72},{64,... | collective-permute-start | bytes 1572872 | tf_op jit(solution)/shard_map/ppermute | solution.py:15
  19.7 58.3 %collective-permute-start.9 = (bf16[128,2048]{0,1:T(8,128)(2,1)S(1)}, bf16[128,2048]{0,1:T(8,128)(2,1)}, u32[]{:S(2)}, u32[]{:S(2)}) collective-permute-start(bf16[128,2048]{0,1:T(8,128)(2,1)S(1)} %bitcast.98), channel_id=1, source_target_pairs={{0,24},{8,32},{16,40},{24,48},{32,56},{40,64},{48,72},{56,80},{64,... | collective-permute-start | bytes 1572872 | tf_op jit(solution)/shard_map/ppermute | solution.py:15
  24.6 18.7 %collective-permute-start.5 = (bf16[16,128]{1,0:T(8,128)(2,1)S(1)}, bf16[16,128]{1,0:T(8,128)(2,1)S(1)}, u32[]{:S(2)}, u32[]{:S(2)}) collective-permute-start(bf16[16,128]{1,0:T(8,128)(2,1)S(1)} %fusion.14), channel_id=1, source_target_pairs={{0,24},{8,32},{16,40},{24,48},{32,56},{40,64},{48,72},{56,80},{64,... | collective-permute-start | bytes 12296 | tf_op jit(solution)/shard_map/ppermute | solution.py:15
  27.3 17.4 %collective-permute-start.4 = (bf16[16,128]{1,0:T(8,128)(2,1)S(1)}, bf16[16,128]{1,0:T(8,128)(2,1)S(1)}, u32[]{:S(2)}, u32[]{:S(2)}) collective-permute-start(bf16[16,128]{1,0:T(8,128)(2,1)S(1)} %fusion.14), channel_id=1, source_target_pairs={{0,32},{8,40},{16,48},{24,56},{32,64},{40,72},{48,80},{56,88},{64,... | collective-permute-start | bytes 12296 | tf_op jit(solution)/shard_map/ppermute | solution.py:15
  43.3 41.0 %collective-permute-start.8 = (bf16[128,2048]{0,1:T(8,128)(2,1)S(1)}, bf16[128,2048]{0,1:T(8,128)(2,1)S(1)}, u32[]{:S(2)}, u32[]{:S(2)}) collective-permute-start(bf16[128,2048]{0,1:T(8,128)(2,1)S(1)} %bitcast.100), channel_id=1, source_target_pairs={{0,32},{8,40},{16,48},{24,56},{32,64},{40,72},{48,80},{56,88},{64,... | collective-permute-start | bytes 1572872 | tf_op jit(solution)/shard_map/ppermute | solution.py:15
  44.7 40.7 %collective-permute-start.3 = (bf16[128,2048]{0,1:T(8,128)(2,1)S(1)}, bf16[128,2048]{0,1:T(8,128)(2,1)}, u32[]{:S(2)}, u32[]{:S(2)}) collective-permute-start(bf16[128,2048]{0,1:T(8,128)(2,1)S(1)} %bitcast.102), channel_id=1, source_target_pairs={{0,8},{8,16},{16,24},{24,32},{32,40},{40,48},{48,56},{56,64},{64,7... | collective-permute-start | bytes 1572872 | tf_op jit(solution)/shard_map/ppermute | solution.py:15
  63.0 24.4 %collective-permute-start.2 = (bf16[128,2048]{0,1:T(8,128)(2,1)S(1)}, bf16[128,2048]{0,1:T(8,128)(2,1)}, u32[]{:S(2)}, u32[]{:S(2)}) collective-permute-start(bf16[128,2048]{0,1:T(8,128)(2,1)S(1)} %bitcast.103), channel_id=1, source_target_pairs={{0,16},{8,24},{16,32},{24,40},{32,48},{40,56},{48,64},{56,72},{64,... | collective-permute-start | bytes 1572872 | tf_op jit(solution)/shard_map/ppermute | solution.py:15
  72.7 20.8 %collective-permute-start.1 = (bf16[128,2048]{0,1:T(8,128)(2,1)S(1)}, bf16[128,2048]{0,1:T(8,128)(2,1)}, u32[]{:S(2)}, u32[]{:S(2)}) collective-permute-start(bf16[128,2048]{0,1:T(8,128)(2,1)S(1)} %bitcast.104), channel_id=1, source_target_pairs={{0,24},{8,32},{16,40},{24,48},{32,56},{40,64},{48,72},{56,80},{64,... | collective-permute-start | bytes 1572872 | tf_op jit(solution)/shard_map/ppermute | solution.py:15
  78.0 17.5 %collective-permute-start = (bf16[128,2048]{0,1:T(8,128)(2,1)S(1)}, bf16[128,2048]{0,1:T(8,128)(2,1)}, u32[]{:S(2)}, u32[]{:S(2)}) collective-permute-start(bf16[128,2048]{0,1:T(8,128)(2,1)S(1)} %bitcast.105), channel_id=1, source_target_pairs={{0,32},{8,40},{16,48},{24,56},{32,64},{40,72},{48,80},{56,88},{64,... | collective-permute-start | bytes 1572872 | tf_op jit(solution)/shard_map/ppermute | solution.py:15
  96.9 6.0 %copy-start.11 = (bf16[128,16,128]{2,0,1:T(8,128)(2,1)S(1)}, bf16[128,16,128]{2,0,1:T(8,128)(2,1)}, u32[]{:S(2)}) copy-start(bf16[128,16,128]{2,0,1:T(8,128)(2,1)} %copy.32) | copy-start | bytes 1572868
  96.9 6.9 %copy-start.10 = (bf16[128,16,128]{2,0,1:T(8,128)(2,1)S(1)}, bf16[128,16,128]{2,0,1:T(8,128)(2,1)}, u32[]{:S(2)}) copy-start(bf16[128,16,128]{2,0,1:T(8,128)(2,1)} %copy.33) | copy-start | bytes 1572868
  112.3 3.5 copy-start.9
  115.8 1.5 copy-start.5
  117.3 3.3 copy-start.6
  126.9 5.2 %copy-start.8 = (bf16[1,128,2048]{1,2,0:T(8,128)(2,1)S(1)}, bf16[1,128,2048]{1,2,0:T(8,128)(2,1)}, u32[]{:S(2)}) copy-start(bf16[1,128,2048]{1,2,0:T(8,128)(2,1)} %copy.76) | copy-start | bytes 1572868
  132.0 1.5 copy-start.2
  141.0 139.2 %copy-start.7 = (bf16[128,16,128]{0,2,1:T(8,128)(2,1)S(1)}, bf16[128,16,128]{0,2,1:T(8,128)(2,1)}, u32[]{:S(2)}) copy-start(bf16[128,16,128]{0,2,1:T(8,128)(2,1)} %copy.55) | copy-start | bytes 1572868
  143.6 153.2 %collective-permute-start.12 = (f32[128,2048]{0,1:T(8,128)}, f32[128,2048]{0,1:T(8,128)}, u32[]{:S(2)}, u32[]{:S(2)}) collective-permute-start(f32[128,2048]{0,1:T(8,128)} %bitcast.111), channel_id=1, source_target_pairs={{8,0},{16,8},{24,16},{32,24},{40,32},{48,40},{56,48},{64,56},{72,6... | collective-permute-start | bytes 3145736 | tf_op jit(solution)/shard_map/ppermute | solution.py:15
  144.8 153.2 %collective-permute-start.13 = (f32[128,2048]{0,1:T(8,128)}, f32[128,2048]{0,1:T(8,128)}, u32[]{:S(2)}, u32[]{:S(2)}) collective-permute-start(f32[128,2048]{0,1:T(8,128)} %bitcast.110), channel_id=1, source_target_pairs={{16,0},{24,8},{32,16},{40,24},{48,32},{56,40},{64,48},{72,56},{80,... | collective-permute-start | bytes 3145736 | tf_op jit(solution)/shard_map/ppermute | solution.py:15
  146.1 153.2 %collective-permute-start.14 = (f32[128,2048]{0,1:T(8,128)}, f32[128,2048]{0,1:T(8,128)}, u32[]{:S(2)}, u32[]{:S(2)}) collective-permute-start(f32[128,2048]{0,1:T(8,128)} %bitcast.108), channel_id=1, source_target_pairs={{24,0},{32,8},{40,16},{48,24},{56,32},{64,40},{72,48},{80,56},{88,... | collective-permute-start | bytes 3145736 | tf_op jit(solution)/shard_map/ppermute | solution.py:15
  147.5 20.4 %collective-permute-start.20 = (f32[16,128]{1,0:T(8,128)S(1)}, f32[16,128]{1,0:T(8,128)S(1)}, u32[]{:S(2)}, u32[]{:S(2)}) collective-permute-start(f32[16,128]{1,0:T(8,128)S(1)} %get-tuple-element.22), channel_id=1, source_target_pairs={{8,0},{16,8},{24,16},{32,24},{40,32},{48,40},{56,48},{64,56},{72,6... | collective-permute-start | bytes 24584 | tf_op jit(solution)/shard_map/ppermute | solution.py:15
  148.8 130.1 %collective-permute-start.23 = (f32[16,128]{1,0:T(8,128)S(1)}, f32[16,128]{1,0:T(8,128)S(1)}, u32[]{:S(2)}, u32[]{:S(2)}) collective-permute-start(f32[16,128]{1,0:T(8,128)S(1)} %get-tuple-element.23), channel_id=1, source_target_pairs={{32,0},{40,8},{48,16},{56,24},{64,32},{72,40},{80,48},{88,56},{96,... | collective-permute-start | bytes 24584 | tf_op jit(solution)/shard_map/ppermute | solution.py:15
  167.9 116.2 %collective-permute-start.22 = (f32[16,128]{1,0:T(8,128)S(1)}, f32[16,128]{1,0:T(8,128)S(1)}, u32[]{:S(2)}, u32[]{:S(2)}) collective-permute-start(f32[16,128]{1,0:T(8,128)S(1)} %get-tuple-element.24), channel_id=1, source_target_pairs={{24,0},{32,8},{40,16},{48,24},{56,32},{64,40},{72,48},{80,56},{88,... | collective-permute-start | bytes 24584 | tf_op jit(solution)/shard_map/ppermute | solution.py:15
  278.9 205.8 %collective-permute-start.15 = (f32[128,2048]{0,1:T(8,128)}, f32[128,2048]{0,1:T(8,128)}, u32[]{:S(2)}, u32[]{:S(2)}) collective-permute-start(f32[128,2048]{0,1:T(8,128)} %bitcast.109), channel_id=1, source_target_pairs={{32,0},{40,8},{48,16},{56,24},{64,32},{72,40},{80,48},{88,56},{96,... | collective-permute-start | bytes 3145736 | tf_op jit(solution)/shard_map/ppermute | solution.py:15
  284.0 11.4 %collective-permute-start.21 = (f32[16,128]{1,0:T(8,128)S(1)}, f32[16,128]{1,0:T(8,128)S(1)}, u32[]{:S(2)}, u32[]{:S(2)}) collective-permute-start(f32[16,128]{1,0:T(8,128)S(1)} %get-tuple-element.25), channel_id=1, source_target_pairs={{16,0},{24,8},{32,16},{40,24},{48,32},{56,40},{64,48},{72,56},{80,... | collective-permute-start | bytes 24584 | tf_op jit(solution)/shard_map/ppermute | solution.py:15
  290.2 10.5 %copy-start.3 = (bf16[16,128,640]{1,2,0:T(8,128)(2,1)S(1)}, bf16[16,128,640]{1,2,0:T(8,128)(2,1)}, u32[]{:S(2)}) copy-start(bf16[16,128,640]{1,2,0:T(8,128)(2,1)} %copy-done.2) | copy-start | bytes 7864324
  295.5 192.7 %collective-permute-start.17 = (f32[128,2048]{1,0:T(8,128)}, f32[128,2048]{1,0:T(8,128)}, u32[]{:S(2)}, u32[]{:S(2)}) collective-permute-start(f32[128,2048]{1,0:T(8,128)} %copy.58), channel_id=1, source_target_pairs={{16,0},{24,8},{32,16},{40,24},{48,32},{56,40},{64,48},{72,56},{80,... | collective-permute-start | bytes 3145736 | tf_op jit(solution)/shard_map/ppermute | solution.py:15
  296.8 191.4 %collective-permute-start.18 = (f32[128,2048]{1,0:T(8,128)}, f32[128,2048]{1,0:T(8,128)}, u32[]{:S(2)}, u32[]{:S(2)}) collective-permute-start(f32[128,2048]{1,0:T(8,128)} %copy.59), channel_id=1, source_target_pairs={{24,0},{32,8},{40,16},{48,24},{56,32},{64,40},{72,48},{80,56},{88,... | collective-permute-start | bytes 3145736 | tf_op jit(solution)/shard_map/ppermute | solution.py:15
  298.1 190.1 %collective-permute-start.19 = (f32[128,2048]{1,0:T(8,128)}, f32[128,2048]{1,0:T(8,128)}, u32[]{:S(2)}, u32[]{:S(2)}) collective-permute-start(f32[128,2048]{1,0:T(8,128)} %copy.60), channel_id=1, source_target_pairs={{32,0},{40,8},{48,16},{56,24},{64,32},{72,40},{80,48},{88,56},{96,... | collective-permute-start | bytes 3145736 | tf_op jit(solution)/shard_map/ppermute | solution.py:15
  299.4 188.7 %collective-permute-start.16 = (f32[128,2048]{1,0:T(8,128)}, f32[128,2048]{1,0:T(8,128)}, u32[]{:S(2)}, u32[]{:S(2)}) collective-permute-start(f32[128,2048]{1,0:T(8,128)} %copy.56), channel_id=1, source_target_pairs={{8,0},{16,8},{24,16},{32,24},{40,32},{48,40},{56,48},{64,56},{72,6... | collective-permute-start | bytes 3145736 | tf_op jit(solution)/shard_map/ppermute | solution.py:15
  303.4 2.6 copy-start.4
  303.5 3.0 copy-start.14
  487.1 4.5 copy-start.1
where the time goes:
time: 493 us; the launch traced here: 492 us
  blocking collectives  178 us (36%)
  waiting for transfers between devices  137 us (28%)
  starting transfers between devices  80.2 us (16%)
  local copies, waits for them, and re-layouts  63.1 us (13%)
  matrix products  20.4 us (4%)
  other arithmetic  10.9 us (2%)
    psum x1, blocking collectives, shards(): bias_total = lax.psum(bias_local, ('seq', 'dp'))  178 us
    ppermute x24, waiting for transfers between devices, passed_along(): lax.ppermute(value, axis, [(source, source + steps) for source in range(f...  137 us
    ppermute x24, starting transfers between devices, passed_along(): lax.ppermute(value, axis, [(source, source + steps) for source in range(f...  80.2 us
    unnamed x48, local copies, waits for them, and re-layouts  20.6 us
    slice x4, local copies, waits for them, and re-layouts, shards(): grad_key[first_row:first_row + tok_rows]  10.2 us
    slice x5, local copies, waits for them, and re-layouts, shards(): grad_value[first_row:first_row + tok_rows]  9.92 us
  transfers between devices with their start and end apart: 24, of which 5 were waited for; matrix products, arithmetic and copies ran while one was open for 8% of the time, Pallas kernels for 0%

commit v1 on v0

--- a/solution.py
+++ b/solution.py
@@ -124,7 +124,7 @@
     query_low = grad_query.reshape(tok_rows, row_width).astype(jnp.bfloat16)
     key_low = key_total.astype(jnp.bfloat16)
     value_low = value_total.astype(jnp.bfloat16)
-    bias_total = lax.psum(bias_local, ("seq", "dp"))
+    bias_total = jnp.sum(lax.all_gather(bias_local, ("seq", "dp")), axis=0)
     return (
         query_low.reshape(1, tok_rows, row_width),
         key_low.reshape(1, tok_rows, row_width),

time: 493 us -> 454 us (0.921)
  the two profiles are of different devices: /device:TPU:1 before, /device:TPU:442 now
where the time goes in v1:
time: 454 us; the launch traced here: 452 us
  waiting for transfers between devices  229 us (50%)
  starting transfers between devices  107 us (24%)
  local copies, waits for them, and re-layouts  62.6 us (14%)
  matrix products  24 us (5%)
  between operations  15.3 us (3%)
  other arithmetic  14.3 us (3%)
    ppermute x24, waiting for transfers between devices, passed_along(): lax.ppermute(value, axis, [(source, source + steps) for source in range(f...  229 us
    ppermute x24, starting transfers between devices, passed_along(): lax.ppermute(value, axis, [(source, source + steps) for source in range(f...  107 us
    unnamed x46, local copies, waits for them, and re-layouts  20.1 us
    slice x4, local copies, waits for them, and re-layouts, shards(): grad_key[first_row:first_row + tok_rows]  10.3 us
    slice x5, local copies, waits for them, and re-layouts, shards(): grad_value[first_row:first_row + tok_rows]  9.92 us
    concatenate x6, local copies, waits for them, and re-layouts, shards(): key_all = jnp.concatenate([arrival[0] for arrival in ordered], axis=0)  9.37 us
  transfers between devices with their start and end apart: 25, of which 9 were waited for; matrix products, arithmetic and copies ran while one was open for 13% of the time, Pallas kernels for 0%

profile of v1, /device:TPU:442, one launch (start us, length us, event | category | flops | bytes accessed | tf_op | source)
XLA Modules:
  0.0 452.4 jit_solution(2023028653008071256)
XLA Ops:
  8.7 2.7 collective-permute-start.7
  11.5 4.5 collective-permute-start.6
  17.3 3.8 collective-permute-start.11
  21.1 2.4 collective-permute-start.10
  23.5 2.8 collective-permute-start.9
  36.8 31.0 %collective-permute-done.5 = bf16[16,128]{1,0:T(8,128)(2,1)S(1)} collective-permute-done((bf16[16,128]{1,0:T(8,128)(2,1)S(1)}, bf16[16,128]{1,0:T(8,128)(2,1)S(1)}, u32[]{:S(2)}, u32[]{:S(2)}) %collective-permute-start.5) | collective-permute-done | bytes 4128 | tf_op jit(solution)/shard_map/ppermute | solution.py:15
  67.8 2.9 collective-permute-start.8
  72.7 7.4 %collective-permute-start.2 = (bf16[128,2048]{0,1:T(8,128)(2,1)S(1)}, bf16[128,2048]{0,1:T(8,128)(2,1)}, u32[]{:S(2)}, u32[]{:S(2)}) collective-permute-start(bf16[128,2048]{0,1:T(8,128)(2,1)S(1)} %bitcast.105), channel_id=1, source_target_pairs={{0,16},{8,24},{16,32},{24,40},{32,48},{40,56},{48,64},{56,72},{64,... | collective-permute-start | bytes 1572872 | tf_op jit(solution)/shard_map/ppermute | solution.py:15
  86.1 2.1 copy.38
  89.2 10.4 %collective-permute-done.3 = bf16[128,2048]{0,1:T(8,128)(2,1)} collective-permute-done((bf16[128,2048]{0,1:T(8,128)(2,1)S(1)}, bf16[128,2048]{0,1:T(8,128)(2,1)}, u32[]{:S(2)}, u32[]{:S(2)}) %collective-permute-start.3) | collective-permute-done | bytes 524320 | tf_op jit(solution)/shard_map/ppermute | solution.py:15
  99.7 2.0 copy.32
  101.7 13.2 %collective-permute-done.2 = bf16[128,2048]{0,1:T(8,128)(2,1)} collective-permute-done((bf16[128,2048]{0,1:T(8,128)(2,1)S(1)}, bf16[128,2048]{0,1:T(8,128)(2,1)}, u32[]{:S(2)}, u32[]{:S(2)}) %collective-permute-start.2) | collective-permute-done | bytes 524320 | tf_op jit(solution)/shard_map/ppermute | solution.py:15
  114.9 2.0 copy.31
  116.9 9.2 %collective-permute-done.1 = bf16[128,2048]{0,1:T(8,128)(2,1)} collective-permute-done((bf16[128,2048]{0,1:T(8,128)(2,1)S(1)}, bf16[128,2048]{0,1:T(8,128)(2,1)}, u32[]{:S(2)}, u32[]{:S(2)}) %collective-permute-start.1) | collective-permute-done | bytes 524320 | tf_op jit(solution)/shard_map/ppermute | solution.py:15
  126.1 2.0 copy.30
  128.1 8.0 %collective-permute-done = bf16[128,2048]{0,1:T(8,128)(2,1)} collective-permute-done((bf16[128,2048]{0,1:T(8,128)(2,1)S(1)}, bf16[128,2048]{0,1:T(8,128)(2,1)}, u32[]{:S(2)}, u32[]{:S(2)}) %collective-permute-start) | collective-permute-done | bytes 524320 | tf_op jit(solution)/shard_map/ppermute | solution.py:15
  139.5 2.0 constant_dynamic-update-slice_fusion.3
  141.5 2.0 constant_dynamic-update-slice_fusion.2
  145.4 7.4 %fusion.34 = (f32[16,128]{1,0:T(8,128)S(1)}, f32[16,128,640]{1,2,0:T(8,128)}) fusion(f32[16,640]{1,0:T(8,128)S(1)} %convert_element_type.46, pred[128,640]{0,1:T(8,128)(4,1)S(1)} %and_and_fusion, bf16[640,16,128]{2,0,1:T(8,128)(2,1)} %constant_dynamic-update-slice_fusion, bf16[128,16,128]{0,2,1:T(8,128)(2,1)} %bitcast.96), kind=kOutput, calls=%fused_computation.67 | convolution fusion | flops 681575040 | bytes 8519680 | tf_op jit(solution)/shard_map/sub | solution.py:82
  157.9 3.3 fusion.8
  163.2 2.6 copy.69
  167.4 6.5 %fusion.35 = (f32[16,640]{1,0:T(8,128)S(1)}, bf16[16,128,640]{1,2,0:T(8,128)(2,1)}) fusion(f32[16,128]{1,0:T(8,128)S(1)} %copy.70, bf16[640,16,128]{2,0,1:T(8,128)(2,1)} %copy-done.4, bf16[128,16,128]{0,2,1:T(8,128)(2,1)} %copy.55, f32[16,128,640]{1,2,0:T(8,128)} %get-tuple-element.27, f32[16,128]{1,0:T(8,128)S(1)} %broadcast_select_fusion), kind=kOutput, calls=%fused_computation.68 | convolution fusion | flops 342087680 | bytes 11067392 | tf_op jit(solution)/shard_map/qhd,khd->hqk/dot_general | solution.py:39
  175.8 2.6 collective-permute-start.23
  178.4 7.0 %collective-permute-start.22 = (f32[16,128]{1,0:T(8,128)S(1)}, f32[16,128]{1,0:T(8,128)S(1)}, u32[]{:S(2)}, u32[]{:S(2)}) collective-permute-start(f32[16,128]{1,0:T(8,128)S(1)} %get-tuple-element.24), channel_id=1, source_target_pairs={{24,0},{32,8},{40,16},{48,24},{56,32},{64,40},{72,48},{80,56},{88,... | collective-permute-start | bytes 24584 | tf_op jit(solution)/shard_map/ppermute | solution.py:15
  185.4 2.1 collective-permute-start.21
  187.6 5.8 %collective-permute-done.21 = f32[16,128]{1,0:T(8,128)S(1)} collective-permute-done((f32[16,128]{1,0:T(8,128)S(1)}, f32[16,128]{1,0:T(8,128)S(1)}, u32[]{:S(2)}, u32[]{:S(2)}) %collective-permute-start.21) | collective-permute-done | bytes 8224 | tf_op jit(solution)/shard_map/ppermute | solution.py:15
  194.3 2.6 multiply_bitcast_fusion
  196.8 2.5 fusion.32
  199.3 2.6 copy.52
  201.9 2.6 copy.51
  204.4 2.6 copy.50
  209.0 2.5 collective-permute-start.13
  211.5 5.1 %collective-permute-start.14 = (f32[128,2048]{0,1:T(8,128)}, f32[128,2048]{0,1:T(8,128)}, u32[]{:S(2)}, u32[]{:S(2)}) collective-permute-start(f32[128,2048]{0,1:T(8,128)} %bitcast.111), channel_id=1, source_target_pairs={{24,0},{32,8},{40,16},{48,24},{56,32},{64,40},{72,48},{80,56},{88,... | collective-permute-start | bytes 3145736 | tf_op jit(solution)/shard_map/ppermute | solution.py:15
  216.6 2.6 copy.53
  219.2 4.1 collective-permute-start.15
  224.4 2.0 fusion.31
  229.1 2.7 copy.59
  231.8 2.6 copy.58
  234.3 4.3 collective-permute-start.17
  238.6 16.7 %collective-permute-done.12 = f32[128,2048]{0,1:T(8,128)} collective-permute-done((f32[128,2048]{0,1:T(8,128)}, f32[128,2048]{0,1:T(8,128)}, u32[]{:S(2)}, u32[]{:S(2)}) %collective-permute-start.12) | collective-permute-done | bytes 1048608 | tf_op jit(solution)/shard_map/ppermute | solution.py:15
  257.2 2.7 collective-permute-start.19
  259.9 35.1 %collective-permute-start.16 = (f32[128,2048]{1,0:T(8,128)}, f32[128,2048]{1,0:T(8,128)}, u32[]{:S(2)}, u32[]{:S(2)}) collective-permute-start(f32[128,2048]{1,0:T(8,128)} %copy.56), channel_id=1, source_target_pairs={{8,0},{16,8},{24,16},{32,24},{40,32},{48,40},{56,48},{64,56},{72,6... | collective-permute-start | bytes 3145736 | tf_op jit(solution)/shard_map/ppermute | solution.py:15
  295.1 2.8 fusion.11
  300.8 2.4 fusion.18
  304.2 32.6 %collective-permute-done.17 = f32[128,2048]{1,0:T(8,128)} collective-permute-done((f32[128,2048]{1,0:T(8,128)}, f32[128,2048]{1,0:T(8,128)}, u32[]{:S(2)}, u32[]{:S(2)}) %collective-permute-start.17) | collective-permute-done | bytes 1048608 | tf_op jit(solution)/shard_map/ppermute | solution.py:15
  336.8 102.0 %collective-permute-done.16 = f32[128,2048]{1,0:T(8,128)} collective-permute-done((f32[128,2048]{1,0:T(8,128)}, f32[128,2048]{1,0:T(8,128)}, u32[]{:S(2)}, u32[]{:S(2)}) %collective-permute-start.16) | collective-permute-done | bytes 1048608 | tf_op jit(solution)/shard_map/ppermute | solution.py:15
  438.8 3.4 fusion.19
  442.2 3.3 reduce_sum.29
  (98 shorter events, 49.7 us)
Async XLA Ops:
  7.2 0.7 copy-start
  7.2 27.3 %copy-start.11 = (bf16[1,128,2048]{2,1,0:T(8,128)(2,1)S(1)}, bf16[1,128,2048]{2,1,0:T(8,128)(2,1)}, u32[]{:S(2)}) copy-start(bf16[1,128,2048]{2,1,0:T(8,128)(2,1)} %param.7) | copy-start | bytes 1572868
  7.2 435.0 %all-gather.3.cloned.1.call-start = ((), (), s32[]{:S(2)}) async-start(), calls=%async_computation | async-start | bytes 4202496 | tf_op jit(solution)/shard_map/all_gather | solution.py:127
  8.7 26.7 %copy-start.12 = (bf16[1,128,2048]{2,1,0:T(8,128)(2,1)S(1)}, bf16[1,128,2048]{2,1,0:T(8,128)(2,1)}, u32[]{:S(2)}) copy-start(bf16[1,128,2048]{2,1,0:T(8,128)(2,1)} %param.10) | copy-start | bytes 1572868
  8.7 18.2 %collective-permute-start.7 = (bf16[16,128]{1,0:T(8,128)(2,1)S(1)}, bf16[16,128]{1,0:T(8,128)(2,1)S(1)}, u32[]{:S(2)}, u32[]{:S(2)}) collective-permute-start(bf16[16,128]{1,0:T(8,128)(2,1)S(1)} %fusion.14), channel_id=1, source_target_pairs={{0,8},{8,16},{16,24},{24,32},{32,40},{40,48},{48,56},{56,64},{64,7... | collective-permute-start | bytes 12296 | tf_op jit(solution)/shard_map/ppermute | solution.py:15
  11.5 17.4 %collective-permute-start.6 = (bf16[16,128]{1,0:T(8,128)(2,1)S(1)}, bf16[16,128]{1,0:T(8,128)(2,1)S(1)}, u32[]{:S(2)}, u32[]{:S(2)}) collective-permute-start(bf16[16,128]{1,0:T(8,128)(2,1)S(1)} %fusion.14), channel_id=1, source_target_pairs={{0,16},{8,24},{16,32},{24,40},{32,48},{40,56},{48,64},{56,72},{64,... | collective-permute-start | bytes 12296 | tf_op jit(solution)/shard_map/ppermute | solution.py:15
  17.3 55.4 %collective-permute-start.11 = (bf16[128,2048]{0,1:T(8,128)(2,1)S(1)}, bf16[128,2048]{0,1:T(8,128)(2,1)S(1)}, u32[]{:S(2)}, u32[]{:S(2)}) collective-permute-start(bf16[128,2048]{0,1:T(8,128)(2,1)S(1)} %bitcast.98), channel_id=1, source_target_pairs={{0,8},{8,16},{16,24},{24,32},{32,40},{40,48},{48,56},{56,64},{64,7... | collective-permute-start | bytes 1572872 | tf_op jit(solution)/shard_map/ppermute | solution.py:15
  21.1 59.0 %collective-permute-start.10 = (bf16[128,2048]{0,1:T(8,128)(2,1)S(1)}, bf16[128,2048]{0,1:T(8,128)(2,1)S(1)}, u32[]{:S(2)}, u32[]{:S(2)}) collective-permute-start(bf16[128,2048]{0,1:T(8,128)(2,1)S(1)} %bitcast.99), channel_id=1, source_target_pairs={{0,16},{8,24},{16,32},{24,40},{32,48},{40,56},{48,64},{56,72},{64,... | collective-permute-start | bytes 1572872 | tf_op jit(solution)/shard_map/ppermute | solution.py:15
  23.5 58.6 %collective-permute-start.9 = (bf16[128,2048]{0,1:T(8,128)(2,1)S(1)}, bf16[128,2048]{0,1:T(8,128)(2,1)}, u32[]{:S(2)}, u32[]{:S(2)}) collective-permute-start(bf16[128,2048]{0,1:T(8,128)(2,1)S(1)} %bitcast.100), channel_id=1, source_target_pairs={{0,24},{8,32},{16,40},{24,48},{32,56},{40,64},{48,72},{56,80},{64,... | collective-permute-start | bytes 1572872 | tf_op jit(solution)/shard_map/ppermute | solution.py:15
  27.0 40.8 %collective-permute-start.5 = (bf16[16,128]{1,0:T(8,128)(2,1)S(1)}, bf16[16,128]{1,0:T(8,128)(2,1)S(1)}, u32[]{:S(2)}, u32[]{:S(2)}) collective-permute-start(bf16[16,128]{1,0:T(8,128)(2,1)S(1)} %fusion.14), channel_id=1, source_target_pairs={{0,24},{8,32},{16,40},{24,48},{32,56},{40,64},{48,72},{56,80},{64,... | collective-permute-start | bytes 12296 | tf_op jit(solution)/shard_map/ppermute | solution.py:15
  28.9 41.8 %collective-permute-start.4 = (bf16[16,128]{1,0:T(8,128)(2,1)S(1)}, bf16[16,128]{1,0:T(8,128)(2,1)S(1)}, u32[]{:S(2)}, u32[]{:S(2)}) collective-permute-start(bf16[16,128]{1,0:T(8,128)(2,1)S(1)} %fusion.14), channel_id=1, source_target_pairs={{0,32},{8,40},{16,48},{24,56},{32,64},{40,72},{48,80},{56,88},{64,... | collective-permute-start | bytes 12296 | tf_op jit(solution)/shard_map/ppermute | solution.py:15
  67.8 20.4 %collective-permute-start.8 = (bf16[128,2048]{0,1:T(8,128)(2,1)S(1)}, bf16[128,2048]{0,1:T(8,128)(2,1)S(1)}, u32[]{:S(2)}, u32[]{:S(2)}) collective-permute-start(bf16[128,2048]{0,1:T(8,128)(2,1)S(1)} %bitcast.102), channel_id=1, source_target_pairs={{0,32},{8,40},{16,48},{24,56},{32,64},{40,72},{48,80},{56,88},{64,... | collective-permute-start | bytes 1572872 | tf_op jit(solution)/shard_map/ppermute | solution.py:15
  70.7 28.9 %collective-permute-start.3 = (bf16[128,2048]{0,1:T(8,128)(2,1)S(1)}, bf16[128,2048]{0,1:T(8,128)(2,1)}, u32[]{:S(2)}, u32[]{:S(2)}) collective-permute-start(bf16[128,2048]{0,1:T(8,128)(2,1)S(1)} %bitcast.104), channel_id=1, source_target_pairs={{0,8},{8,16},{16,24},{24,32},{32,40},{40,48},{48,56},{56,64},{64,7... | collective-permute-start | bytes 1572872 | tf_op jit(solution)/shard_map/ppermute | solution.py:15
  72.7 42.2 %collective-permute-start.2 = (bf16[128,2048]{0,1:T(8,128)(2,1)S(1)}, bf16[128,2048]{0,1:T(8,128)(2,1)}, u32[]{:S(2)}, u32[]{:S(2)}) collective-permute-start(bf16[128,2048]{0,1:T(8,128)(2,1)S(1)} %bitcast.105), channel_id=1, source_target_pairs={{0,16},{8,24},{16,32},{24,40},{32,48},{40,56},{48,64},{56,72},{64,... | collective-permute-start | bytes 1572872 | tf_op jit(solution)/shard_map/ppermute | solution.py:15
  80.1 46.0 %collective-permute-start.1 = (bf16[128,2048]{0,1:T(8,128)(2,1)S(1)}, bf16[128,2048]{0,1:T(8,128)(2,1)}, u32[]{:S(2)}, u32[]{:S(2)}) collective-permute-start(bf16[128,2048]{0,1:T(8,128)(2,1)S(1)} %bitcast.106), channel_id=1, source_target_pairs={{0,24},{8,32},{16,40},{24,48},{32,56},{40,64},{48,72},{56,80},{64,... | collective-permute-start | bytes 1572872 | tf_op jit(solution)/shard_map/ppermute | solution.py:15
  82.1 54.1 %collective-permute-start = (bf16[128,2048]{0,1:T(8,128)(2,1)S(1)}, bf16[128,2048]{0,1:T(8,128)(2,1)}, u32[]{:S(2)}, u32[]{:S(2)}) collective-permute-start(bf16[128,2048]{0,1:T(8,128)(2,1)S(1)} %bitcast.107), channel_id=1, source_target_pairs={{0,32},{8,40},{16,48},{24,56},{32,64},{40,72},{48,80},{56,88},{64,... | collective-permute-start | bytes 1572872 | tf_op jit(solution)/shard_map/ppermute | solution.py:15
  137.5 6.1 %copy-start.10 = (bf16[128,16,128]{2,0,1:T(8,128)(2,1)S(1)}, bf16[128,16,128]{2,0,1:T(8,128)(2,1)}, u32[]{:S(2)}) copy-start(bf16[128,16,128]{2,0,1:T(8,128)(2,1)} %copy.32) | copy-start | bytes 1572868
  137.5 7.0 %copy-start.9 = (bf16[128,16,128]{2,0,1:T(8,128)(2,1)S(1)}, bf16[128,16,128]{2,0,1:T(8,128)(2,1)}, u32[]{:S(2)}) copy-start(bf16[128,16,128]{2,0,1:T(8,128)(2,1)} %copy.33) | copy-start | bytes 1572868
  152.8 3.5 copy-start.8
  156.4 1.6 copy-start.4
  157.9 3.3 copy-start.5
  167.4 26.0 %copy-start.13 = (s32[1,128]{1,0:T(1,128)S(1)}, s32[1,128]{1,0:T(1,128)}, u32[]{:S(2)}) copy-start(s32[1,128]{1,0:T(1,128)} %param.12) | copy-start | bytes 1540
  167.4 26.8 %copy-start.7 = (bf16[1,128,2048]{1,2,0:T(8,128)(2,1)S(1)}, bf16[1,128,2048]{1,2,0:T(8,128)(2,1)}, u32[]{:S(2)}) copy-start(bf16[1,128,2048]{1,2,0:T(8,128)(2,1)} %copy.76) | copy-start | bytes 1572868
  173.9 13.6 %collective-permute-start.20 = (f32[16,128]{1,0:T(8,128)S(1)}, f32[16,128]{1,0:T(8,128)S(1)}, u32[]{:S(2)}, u32[]{:S(2)}) collective-permute-start(f32[16,128]{1,0:T(8,128)S(1)} %get-tuple-element.22), channel_id=1, source_target_pairs={{8,0},{16,8},{24,16},{32,24},{40,32},{48,40},{56,48},{64,56},{72,6... | collective-permute-start | bytes 24584 | tf_op jit(solution)/shard_map/ppermute | solution.py:15
  175.8 11.7 %collective-permute-start.23 = (f32[16,128]{1,0:T(8,128)S(1)}, f32[16,128]{1,0:T(8,128)S(1)}, u32[]{:S(2)}, u32[]{:S(2)}) collective-permute-start(f32[16,128]{1,0:T(8,128)S(1)} %get-tuple-element.23), channel_id=1, source_target_pairs={{32,0},{40,8},{48,16},{56,24},{64,32},{72,40},{80,48},{88,56},{96,... | collective-permute-start | bytes 24584 | tf_op jit(solution)/shard_map/ppermute | solution.py:15
  178.4 9.2 %collective-permute-start.22 = (f32[16,128]{1,0:T(8,128)S(1)}, f32[16,128]{1,0:T(8,128)S(1)}, u32[]{:S(2)}, u32[]{:S(2)}) collective-permute-start(f32[16,128]{1,0:T(8,128)S(1)} %get-tuple-element.24), channel_id=1, source_target_pairs={{24,0},{32,8},{40,16},{48,24},{56,32},{64,40},{72,48},{80,56},{88,... | collective-permute-start | bytes 24584 | tf_op jit(solution)/shard_map/ppermute | solution.py:15
  185.4 7.9 %collective-permute-start.21 = (f32[16,128]{1,0:T(8,128)S(1)}, f32[16,128]{1,0:T(8,128)S(1)}, u32[]{:S(2)}, u32[]{:S(2)}) collective-permute-start(f32[16,128]{1,0:T(8,128)S(1)} %get-tuple-element.25), channel_id=1, source_target_pairs={{16,0},{24,8},{32,16},{40,24},{48,32},{56,40},{64,48},{72,56},{80,... | collective-permute-start | bytes 24584 | tf_op jit(solution)/shard_map/ppermute | solution.py:15
  204.4 18.9 %copy-start.6 = (bf16[128,16,128]{0,2,1:T(8,128)(2,1)S(1)}, bf16[128,16,128]{0,2,1:T(8,128)(2,1)}, u32[]{:S(2)}) copy-start(bf16[128,16,128]{0,2,1:T(8,128)(2,1)} %copy.55) | copy-start | bytes 1572868
  207.1 48.2 %collective-permute-start.12 = (f32[128,2048]{0,1:T(8,128)}, f32[128,2048]{0,1:T(8,128)}, u32[]{:S(2)}, u32[]{:S(2)}) collective-permute-start(f32[128,2048]{0,1:T(8,128)} %bitcast.113), channel_id=1, source_target_pairs={{8,0},{16,8},{24,16},{32,24},{40,32},{48,40},{56,48},{64,56},{72,6... | collective-permute-start | bytes 3145736 | tf_op jit(solution)/shard_map/ppermute | solution.py:15
  209.0 48.2 %collective-permute-start.13 = (f32[128,2048]{0,1:T(8,128)}, f32[128,2048]{0,1:T(8,128)}, u32[]{:S(2)}, u32[]{:S(2)}) collective-permute-start(f32[128,2048]{0,1:T(8,128)} %bitcast.112), channel_id=1, source_target_pairs={{16,0},{24,8},{32,16},{40,24},{48,32},{56,40},{64,48},{72,56},{80,... | collective-permute-start | bytes 3145736 | tf_op jit(solution)/shard_map/ppermute | solution.py:15
  211.5 48.4 %collective-permute-start.14 = (f32[128,2048]{0,1:T(8,128)}, f32[128,2048]{0,1:T(8,128)}, u32[]{:S(2)}, u32[]{:S(2)}) collective-permute-start(f32[128,2048]{0,1:T(8,128)} %bitcast.111), channel_id=1, source_target_pairs={{24,0},{32,8},{40,16},{48,24},{56,32},{64,40},{72,48},{80,56},{88,... | collective-permute-start | bytes 3145736 | tf_op jit(solution)/shard_map/ppermute | solution.py:15
  219.2 81.6 %collective-permute-start.15 = (f32[128,2048]{0,1:T(8,128)}, f32[128,2048]{0,1:T(8,128)}, u32[]{:S(2)}, u32[]{:S(2)}) collective-permute-start(f32[128,2048]{0,1:T(8,128)} %bitcast.110), channel_id=1, source_target_pairs={{32,0},{40,8},{48,16},{56,24},{64,32},{72,40},{80,48},{88,56},{96,... | collective-permute-start | bytes 3145736 | tf_op jit(solution)/shard_map/ppermute | solution.py:15
  229.1 66.0 %copy-start.2 = (bf16[16,128,640]{1,2,0:T(8,128)(2,1)S(1)}, bf16[16,128,640]{1,2,0:T(8,128)(2,1)}, u32[]{:S(2)}) copy-start(bf16[16,128,640]{1,2,0:T(8,128)(2,1)} %get-tuple-element.29) | copy-start | bytes 7864324
  234.3 102.4 %collective-permute-start.17 = (f32[128,2048]{1,0:T(8,128)}, f32[128,2048]{1,0:T(8,128)}, u32[]{:S(2)}, u32[]{:S(2)}) collective-permute-start(f32[128,2048]{1,0:T(8,128)} %copy.58), channel_id=1, source_target_pairs={{16,0},{24,8},{32,16},{40,24},{48,32},{56,40},{64,48},{72,56},{80,... | collective-permute-start | bytes 3145736 | tf_op jit(solution)/shard_map/ppermute | solution.py:15
  255.2 81.5 %collective-permute-start.18 = (f32[128,2048]{1,0:T(8,128)}, f32[128,2048]{1,0:T(8,128)}, u32[]{:S(2)}, u32[]{:S(2)}) collective-permute-start(f32[128,2048]{1,0:T(8,128)} %copy.59), channel_id=1, source_target_pairs={{24,0},{32,8},{40,16},{48,24},{56,32},{64,40},{72,48},{80,56},{88,... | collective-permute-start | bytes 3145736 | tf_op jit(solution)/shard_map/ppermute | solution.py:15
  257.2 79.6 %collective-permute-start.19 = (f32[128,2048]{1,0:T(8,128)}, f32[128,2048]{1,0:T(8,128)}, u32[]{:S(2)}, u32[]{:S(2)}) collective-permute-start(f32[128,2048]{1,0:T(8,128)} %copy.60), channel_id=1, source_target_pairs={{32,0},{40,8},{48,16},{56,24},{64,32},{72,40},{80,48},{88,56},{96,... | collective-permute-start | bytes 3145736 | tf_op jit(solution)/shard_map/ppermute | solution.py:15
  259.9 178.9 %collective-permute-start.16 = (f32[128,2048]{1,0:T(8,128)}, f32[128,2048]{1,0:T(8,128)}, u32[]{:S(2)}, u32[]{:S(2)}) collective-permute-start(f32[128,2048]{1,0:T(8,128)} %copy.56), channel_id=1, source_target_pairs={{8,0},{16,8},{24,16},{32,24},{40,32},{48,40},{56,48},{64,56},{72,6... | collective-permute-start | bytes 3145736 | tf_op jit(solution)/shard_map/ppermute | solution.py:15
  297.8 2.6 copy-start.3
  438.8 6.8 %copy-start.1 = (bf16[16,64]{1,0:T(8,128)(2,1)S(1)}, bf16[16,64]{1,0:T(8,128)(2,1)}, u32[]{:S(2)}) copy-start(bf16[16,64]{1,0:T(8,128)(2,1)} %param.13) | copy-start | bytes 6148
Sparse Core Ops, SparseCore 0:
  194.4 216.3 all-gather.2
